TPU v7x, 32 devices: a whole 2x2x4 slice. The times are simulated.
32 devices in a mesh: tok: 16 (over z, y, x), head: 2 (over core).
Axes of the slice: x: 2, y: 2, z: 4, core: 2. Of those that a mesh axis runs over, the one named last changes fastest.
Arguments:
- queries: bfloat16 [2, 4096, 512], P('head', 'tok'), may hold values from -6 to 6
- key_rows: bfloat16 [2, 4096, 512], P('head', 'tok'), may hold values from -6 to 6
- value_rows: bfloat16 [2, 4096, 512], P('head', 'tok'), may hold values from -6 to 6
- step_rates: float32 [2, 4096], P('head', 'tok'), may hold values from 0.1 to 1
- w_gate: bfloat16 [2, 512, 512], P('head'), may hold values from -0.25 to 0.25
- w_up: bfloat16 [2, 512, 512], P('head'), may hold values from -0.25 to 0.25
- w_down: bfloat16 [2, 512, 512], P('head'), may hold values from -0.25 to 0.25
- out_gain: float32 [2, 512], P('head'), may hold values from 0.1 to 1.9
- cotangent: bfloat16 [2, 4096, 512], P('head', 'tok'), may hold values from -6 to 6
Outputs:
- grad_queries: bfloat16 [2, 4096, 512], P('head', 'tok')
- grad_keys: bfloat16 [2, 4096, 512], P('head', 'tok')
- grad_values: bfloat16 [2, 4096, 512], P('head', 'tok')
- grad_gate: float32 [2, 512, 512], P('head', 'tok')
- grad_up: float32 [2, 512, 512], P('head', 'tok')
- grad_down: float32 [2, 512, 512], P('head', 'tok')
All inputs are finite; a program needn't handle non-finite values.
Results may differ from a plain program's by a relative error of at most 0.03.
Values sent between devices are 32-bit elements; how exact they have to be, the bound alone decides.
A program may use at most 128 MiB of HBM per device.

v0:
```python
import jax
import jax.numpy as jnp
from jax import lax
from jax.sharding import PartitionSpec as P

NS_STEPS = 3
coef_first = 3.4445
coef_second = -4.775
coef_third = 2.0315
inner_step = 0.5


def contract_rows(first_op, second_op):
    return lax.dot_general(
        first_op, second_op, (((0,), (0,)), ((), ())), preferred_element_type=jnp.float32
    )


def contract_cols(first_op, second_op):
    return lax.dot_general(
        first_op, second_op, (((1,), (1,)), ((), ())), preferred_element_type=jnp.float32
    )


def silu_parts(pre_gate):
    sigma_gate = jax.nn.sigmoid(pre_gate)
    act_gate = pre_gate * sigma_gate
    slope_gate = sigma_gate * (1.0 + pre_gate * (1.0 - sigma_gate))
    return (act_gate, slope_gate, sigma_gate)


def orthogonalize(matrix):
    current = matrix / jnp.sqrt(jnp.sum(matrix * matrix) + 1e-06)
    for iteration in range(NS_STEPS):
        narrow = current.astype(jnp.bfloat16)
        gram_matrix = contract_cols(narrow, narrow)
        gram_low = gram_matrix.astype(jnp.bfloat16)
        poly_term = (
            coef_second * gram_matrix
            + coef_third * jnp.dot(gram_low, gram_low, preferred_element_type=jnp.float32)
        ).astype(jnp.bfloat16)
        current = coef_first * current + jnp.dot(
            poly_term, narrow, preferred_element_type=jnp.float32
        )
    return current


def orthogonalize_all(grad_triple):
    mapped = jax.vmap(orthogonalize)
    return (mapped(grad_triple[0]), mapped(grad_triple[1]), mapped(grad_triple[2]))


def key_forward(w_gate, w_up, w_down, key_rows, value_rows, step_rates):
    key_gate = jnp.dot(key_rows, w_gate, preferred_element_type=jnp.float32)
    key_up = jnp.dot(key_rows, w_up, preferred_element_type=jnp.float32)
    act_gate, slope_gate, sigma_gate = silu_parts(key_gate)
    key_mixed = (act_gate * key_up).astype(jnp.bfloat16)
    target = (-step_rates[:, None] * value_rows).astype(jnp.bfloat16)
    key_mid = contract_cols(target, w_down)
    key_dgate = (key_mid * key_up * slope_gate).astype(jnp.bfloat16)
    key_dup = (key_mid * act_gate).astype(jnp.bfloat16)
    inner_grads = (
        contract_rows(key_rows, key_dgate),
        contract_rows(key_rows, key_dup),
        contract_rows(key_mixed, target),
    )
    stored = (
        key_gate,
        key_up,
        act_gate,
        slope_gate,
        sigma_gate,
        key_mixed,
        target,
        key_mid,
        key_dgate,
        key_dup,
    )
    return (inner_grads, stored)


def key_backward(w_gate, w_up, w_down, key_rows, step_rates, stored, back_a, back_b, back_c):
    (
        key_gate,
        key_up,
        act_gate,
        slope_gate,
        sigma_gate,
        key_mixed,
        target,
        key_mid,
        key_dgate,
        key_dup,
    ) = stored
    cot_a = back_a.astype(jnp.bfloat16)
    cot_b = back_b.astype(jnp.bfloat16)
    cot_c = back_c.astype(jnp.bfloat16)
    back_gate = jnp.dot(key_rows, cot_a, preferred_element_type=jnp.float32)
    back_up = jnp.dot(key_rows, cot_b, preferred_element_type=jnp.float32)
    back_mixed = contract_cols(target, cot_c)
    back_target = jnp.dot(key_mixed, cot_c, preferred_element_type=jnp.float32)
    curve_gate = sigma_gate * (1.0 - sigma_gate) * (2.0 + key_gate * (1.0 - 2.0 * sigma_gate))
    back_mid = (back_gate * key_up * slope_gate + back_up * act_gate).astype(jnp.bfloat16)
    gate_back = (
        back_gate * key_mid * key_up * curve_gate
        + back_up * key_mid * slope_gate
        + back_mixed * key_up * slope_gate
    ).astype(jnp.bfloat16)
    up_back = (back_gate * key_mid * slope_gate + back_mixed * act_gate).astype(jnp.bfloat16)
    key_grad = (
        contract_cols(key_dgate, cot_a)
        + contract_cols(key_dup, cot_b)
        + contract_cols(gate_back, w_gate)
        + contract_cols(up_back, w_up)
    )
    value_sum = back_target + jnp.dot(back_mid, w_down, preferred_element_type=jnp.float32)
    value_grad = (-step_rates[:, None] * value_sum).astype(jnp.bfloat16)
    weight_terms = jnp.concatenate(
        [
            contract_rows(key_rows, gate_back),
            contract_rows(key_rows, up_back),
            contract_rows(back_mid, target),
        ],
        axis=1,
    )
    return (key_grad.astype(jnp.bfloat16), value_grad, weight_terms)


def query_forward(new_gate, new_up, new_down, queries):
    query_gate = jnp.dot(queries, new_gate, preferred_element_type=jnp.float32)
    query_up = jnp.dot(queries, new_up, preferred_element_type=jnp.float32)
    act_gate, slope_gate, sigma_gate = silu_parts(query_gate)
    query_mixed = (act_gate * query_up).astype(jnp.bfloat16)
    output = jnp.dot(query_mixed, new_down, preferred_element_type=jnp.float32)
    return (output, (query_up, act_gate, slope_gate, query_mixed))


def query_backward(new_gate, new_up, new_down, queries, stored, grad_output):
    query_up, act_gate, slope_gate, query_mixed = stored
    query_mid = contract_cols(grad_output, new_down)
    query_dgate = (query_mid * query_up * slope_gate).astype(jnp.bfloat16)
    query_dup = (query_mid * act_gate).astype(jnp.bfloat16)
    query_grad = (contract_cols(query_dgate, new_gate) + contract_cols(query_dup, new_up)).astype(
        jnp.bfloat16
    )
    weight_terms = jnp.concatenate(
        [
            contract_rows(queries, query_dgate),
            contract_rows(queries, query_dup),
            contract_rows(query_mixed, grad_output),
        ],
        axis=1,
    )
    return (query_grad, weight_terms)


def local(queries, key_rows, value_rows, step_rates, w_gate, w_up, w_down, out_gain, cotangent):
    head_size = w_gate.shape[2]
    local_grads, stored = jax.vmap(key_forward)(
        w_gate, w_up, w_down, key_rows, value_rows, step_rates
    )
    inner_grads = lax.psum((local_grads[0], local_grads[1], local_grads[2]), "tok")
    unitary, ns_back = jax.vjp(orthogonalize_all, inner_grads)
    new_gate = (w_gate - inner_step * unitary[0]).astype(jnp.bfloat16)
    new_up = (w_up - inner_step * unitary[1]).astype(jnp.bfloat16)
    new_down = (w_down - inner_step * unitary[2]).astype(jnp.bfloat16)
    output, query_stored = jax.vmap(query_forward)(new_gate, new_up, new_down, queries)
    full_width = queries.shape[0] * lax.axis_size("head") * head_size
    squares_local = jnp.sum(output * output, axis=(0, 2))
    gain_wide = out_gain[:, None, :]
    squares, aligned = lax.psum(
        (squares_local, jnp.sum(cotangent * gain_wide * output, axis=(0, 2))), "head"
    )
    inverse_rms = lax.rsqrt(squares / full_width + 1e-05)
    grad_output = (
        gain_wide * cotangent * inverse_rms[None, :, None]
        - output * (aligned * inverse_rms * inverse_rms * inverse_rms / full_width)[None, :, None]
    ).astype(jnp.bfloat16)
    query_grad, query_terms = jax.vmap(query_backward)(
        new_gate, new_up, new_down, queries, query_stored, grad_output
    )
    share_rows = head_size // lax.axis_size("tok")
    query_whole = lax.psum(query_terms, "tok")
    query_share = lax.dynamic_slice_in_dim(
        query_whole, lax.axis_index("tok") * share_rows, share_rows, 1
    )
    outer_back = (
        -inner_step * query_whole[:, :, :head_size],
        -inner_step * query_whole[:, :, head_size : 2 * head_size],
        -inner_step * query_whole[:, :, 2 * head_size :],
    )
    back_triple = ns_back(outer_back)[0]
    key_grad, value_grad, key_terms = jax.vmap(key_backward)(
        w_gate,
        w_up,
        w_down,
        key_rows,
        step_rates,
        stored,
        back_triple[0],
        back_triple[1],
        back_triple[2],
    )
    key_share = lax.psum_scatter(key_terms, "tok", scatter_dimension=1, tiled=True)
    weight_share = query_share + key_share
    return (
        query_grad,
        key_grad,
        value_grad,
        weight_share[:, :, :head_size],
        weight_share[:, :, head_size : 2 * head_size],
        weight_share[:, :, 2 * head_size :],
    )


def solution(mesh):
    in_specs = (
        P("head", "tok", None),
        P("head", "tok", None),
        P("head", "tok", None),
        P("head", "tok"),
        P("head", None, None),
        P("head", None, None),
        P("head", None, None),
        P("head", None),
        P("head", "tok", None),
    )
    out_specs = (
        P("head", "tok", None),
        P("head", "tok", None),
        P("head", "tok", None),
        P("head", "tok", None),
        P("head", "tok", None),
        P("head", "tok", None),
    )
    return jax.shard_map(local, mesh=mesh, in_specs=in_specs, out_specs=out_specs, check_vma=False)
```

profile of v0, /device:TPU:0, one launch (start us, length us, event | category | flops | bytes accessed | tf_op | source)
XLA Modules:
  0.0 571.0 jit_solution(9727249518634274139)
XLA Ops:
  7.2 0.7 neg.32
  8.1 1.3 fusion.266
  9.5 1.6 fusion.272
  11.1 2.4 multiply_convert_fusion.2
  13.6 1.3 convolution_bitcast_fusion.8
  14.9 1.4 convolution_bitcast_fusion.7
  16.3 1.4 convolution_bitcast_fusion.6
  17.8 1.1 copy.62
  18.9 1.1 copy.67
  20.0 1.0 copy.72
  21.0 146.9 %all-reduce.11.cloned.1.call-done = (f32[1,512,512]{1,2,0:T(8,128)}, f32[1,512,512]{1,2,0:T(8,128)}, f32[1,512,512]{1,2,0:T(8,128)}) async-done(((f32[1,512,512]{1,2,0:T(8,128)}, f32[1,512,512]{1,2,0:T(8,128)}, f32[1,512,512]{1,2,0:T(8,128)}), (f32[1,512,512]{1,2,0:T(8,128)}, f32[1,512,512]{1,2,0:T(8,128)}, f32[1,512,512]{1,2,0:T(8,128)})) %all-reduce.11.cloned.1.call-update) | async-done | bytes 3145744 | tf_op jit(solution)/shard_map/psum | solution.py:162
  167.9 2.1 multiply_reduce_fusion.5
  170.7 2.2 fusion.263
  175.1 0.8 copy-done.68
  176.9 1.3 fusion.26
  178.2 0.9 multiply_reduce_fusion.4
  180.7 0.8 copy-done.97
  183.0 0.8 copy-done.64
  184.7 1.2 fusion.29
  186.0 0.9 multiply_reduce_fusion.3
  188.5 0.8 copy-done.95
  190.7 0.8 copy-done.60
  193.0 0.5 fusion.36
  194.4 0.5 fusion.37
  194.9 1.2 multiply_convert_fusion.3
  196.1 0.5 fusion.38
  197.1 0.8 copy-done.28
  198.0 2.5 all-reduce.2
  200.5 1.3 fusion.304
  201.8 1.3 convolution_bitcast_fusion.3
  203.1 1.8 multiply_convert_fusion
  206.0 2.0 pad_maximum_fusion
  208.5 145.7 %all-reduce.7.cloned.1.call-done = f32[1,512,1536]{1,2,0:T(8,128)} async-done(((f32[1,512,1536]{1,2,0:T(8,128)}), f32[1,512,1536]{1,2,0:T(8,128)}) %all-reduce.7.cloned.1.call-update) | async-done | bytes 3145744 | tf_op jit(solution)/shard_map/psum | solution.py:183
  354.2 1.8 convolution_convert_fusion.52
  356.1 1.7 fusion.39
  370.9 1.2 fusion.72
  372.1 1.3 convolution_convert_fusion.22
  375.4 0.7 fusion.135
  379.9 1.2 fusion.81
  381.1 1.3 convolution_convert_fusion.4
  383.9 2.2 multiply_reduce_fusion.2
  386.7 1.9 fusion.49
  388.6 2.0 fusion.103
  391.1 0.8 copy-done.45
  391.9 2.1 multiply_reduce_fusion.1
  394.7 3.0 fusion.172
  397.7 1.1 convolution_bitcast_fusion.19
  399.4 0.5 fusion.91
  400.4 0.8 copy-done.43
  401.1 1.3 multiply_reduce_fusion
  404.9 0.7 add_convert_fusion
  407.2 5.7 copy.106
  412.9 0.6 copy-done.104
  413.5 0.6 dynamic-slice
  414.8 1.3 fusion.455
  416.1 2.0 fusion.161
  419.2 1.0 fusion.160
  420.6 1.0 fusion.162
  421.6 137.6 %all-reduce.9.cloned.1.call-done = f32[1,512,1536]{2,0,1:T(1,128)} async-done(((f32[1,512,1536]{2,0,1:T(1,128)}), f32[1,512,1536]{2,0,1:T(1,128)}) %all-reduce.9.cloned.1.call-update) | async-done | bytes 3145744
  559.2 0.9 constant_dynamic-slice_fusion
  560.4 1.4 dynamic-slice_add_fusion
  561.9 0.7 copy.108
  562.6 0.7 copy.109
  563.4 0.7 copy.110
  (289 shorter events, 39.2 us)
Async XLA Ops:
  7.2 160.8 %all-reduce.11.cloned.1.call-start = ((), (), s32[]{:S(2)}) async-start(), calls=%async_computation.2 | async-start | bytes 6291456 | tf_op jit(solution)/shard_map/psum | solution.py:162
  9.5 5.4 copy-start.89
  11.1 5.2 copy-start.91
  11.1 5.2 copy-start.46
  13.6 2.7 copy-start.75
  13.6 2.7 copy-start.73
  13.6 2.7 copy-start.77
  14.9 2.9 copy-start.20
  16.3 2.6 copy-start.54
  16.3 3.7 copy-start.29
  17.8 336.4 %all-reduce.7.cloned.1.call-start = ((), (), s32[]{:S(2)}) async-start(), calls=%async_computation | async-start | bytes 6291456 | tf_op jit(solution)/shard_map/psum | solution.py:183
  170.7 2.6 copy-start.33
  174.2 2.2 copy-start.6
  174.6 2.2 copy-start.14
  175.9 2.3 copy-start.35
  180.2 1.8 copy-start.39
  182.0 2.2 copy-start.4
  182.5 2.2 copy-start.10
  183.7 2.2 copy-start.31
  189.8 2.2 copy-start.2
  190.2 2.3 copy-start.8
  192.5 2.4 copy-start.12
  192.5 1.8 copy-start.66
  193.0 3.1 copy-start.62
  193.6 2.5 copy-start.22
  194.3 2.3 copy-start.94
  194.3 1.7 copy-start.56
  194.9 2.2 copy-start.50
  194.9 1.8 copy-start.82
  194.9 1.8 copy-start.103
  196.1 1.9 copy-start.88
  200.5 4.4 copy-start.49
  208.0 351.1 %all-reduce.9.cloned.1.call-start = ((), (), s32[]{:S(2)}) async-start(), calls=%async_computation.1 | async-start | bytes 6291456
  354.2 3.6 copy-start.19
  354.2 4.1 copy-start.1
  354.2 4.1 copy-start.71
  364.3 1.8 copy-start.67
  370.3 1.8 copy-start.36
  370.9 2.5 copy-start.44
  372.1 1.8 copy-start.13
  379.3 1.8 copy-start.32
  379.9 2.5 copy-start.42
  379.9 2.5 copy-start.41
  386.7 4.0 copy-start.102
  394.7 4.2 copy-start.38
  394.7 4.2 copy-start.72
  397.7 2.6 copy-start.24
  397.7 2.2 copy-start.101
  401.1 2.3 copy-start.47
  403.5 2.2 copy-start.26
  412.8 1.9 copy-start.23
  412.9 3.2 copy-start.51
  412.9 5.3 copy-start.25
  412.9 5.3 copy-start.78
  412.9 5.6 copy-start.53
  412.9 5.6 copy-start.76
  412.9 5.9 %copy-start.21 = (bf16[1,512,512]{2,1,0:T(8,128)(2,1)S(1)}, bf16[1,512,512]{2,1,0:T(8,128)(2,1)}, u32[]{:S(2)}) copy-start(bf16[1,512,512]{2,1,0:T(8,128)(2,1)} %param.13) | copy-start | bytes 1572868
  414.8 4.0 copy-start.81
  416.1 3.1 copy-start.55
  416.1 3.1 copy-start.87
  418.1 2.1 copy-start.27
  418.1 2.1 copy-start.74
  418.4 2.1 copy-start.30
  418.5 2.1 copy-start.85
  (45 other events, 51.4 us)
Sparse Core Ops, SparseCore 0:
  17.9 149.9 all-reduce.10
  208.2 146.0 all-reduce.6
  413.0 146.1 all-reduce.8
where the time goes:
time: 582 us; the launch traced here: 571 us
  waiting for transfers between devices  430 us (74%)
  matrix products  79.5 us (14%)
  local copies, waits for them, and re-layouts  24.8 us (4%)
  between operations  20.8 us (4%)
  other arithmetic  12.9 us (2%)
    psum x1, waiting for transfers between devices, local(): lax.psum((local_grads[0], local_grads[1], local_grads[2]), 'tok')  147 us
    psum x1, waiting for transfers between devices, local(): query_whole = lax.psum(query_terms, 'tok')  146 us
    unnamed x4, waiting for transfers between devices  138 us
    dot_general x36, matrix products, contract_cols(): lax.dot_general(first_op, second_op, (((1,), (1,)), ((), ())), preferred_...  27.5 us
    unnamed x220, local copies, waits for them, and re-layouts  18.8 us
    dot_general x27, matrix products, orthogonalize(): jnp.dot(gram_low, gram_low, preferred_element_type=jnp.float32)  18.8 us
    dot_general x27, matrix products, orthogonalize(): jnp.dot(poly_term, narrow, preferred_element_type=jnp.float32)  17.2 us
  transfers between devices with their start and end apart: 3, of which 3 were waited for; matrix products, arithmetic and copies ran while one was open for 2% of the time, Pallas kernels for 0%

commit v1 on v0

--- a/solution.py
+++ b/solution.py
@@ -180,7 +180,7 @@
         new_gate, new_up, new_down, queries, query_stored, grad_output
     )
     share_rows = head_size // lax.axis_size("tok")
-    query_whole = lax.psum(query_terms, "tok")
+    query_whole = jnp.sum(lax.all_gather(query_terms, "tok"), axis=0)
     query_share = lax.dynamic_slice_in_dim(
         query_whole, lax.axis_index("tok") * share_rows, share_rows, 1
     )

time: 582 us -> 973 us (1.67)
  waiting for transfers between devices: 430 us -> 791 us
  other arithmetic: 12.9 us -> 30.2 us
  blocking collectives: 2.47 us -> 13.2 us
    all_gather x0 -> x1, waiting for transfers between devices: none -> 508 us  [local(): query_whole = jnp.sum(lax.all_gather(query_terms, 'tok'), axis=0)]
    psum x1 -> x0, waiting for transfers between devices: 146 us -> none  [local(): query_whole = lax.psum(query_terms, 'tok')]
    reduce_sum x0 -> x1, other arithmetic: none -> 20.5 us  [local(): query_whole = jnp.sum(lax.all_gather(query_terms, 'tok'), axis=0)]
    psum x1, blocking collectives: 2.47 us -> 13.2 us  [local(): lax.psum((squares_local, jnp.sum(cotangent * gain_wide * output, axis=(0,...]
  transfers between devices with their start and end apart: 3 -> 3, of which waited for: 3 -> 3; matrix products, arithmetic and copies ran while one was open for 2% -> 1% of each run, Pallas kernels for 0% -> 0%
where the time goes in v1:
time: 973 us; the launch traced here: 963 us
  waiting for transfers between devices  791 us (81%)
  matrix products  77.1 us (8%)
  local copies, waits for them, and re-layouts  30.2 us (3%)
  other arithmetic  30.2 us (3%)
  between operations  20.9 us (2%)
  blocking collectives  13.2 us (1%)
    all_gather x1, waiting for transfers between devices, local(): query_whole = jnp.sum(lax.all_gather(query_terms, 'tok'), axis=0)  508 us
    psum x1, waiting for transfers between devices, local(): lax.psum((local_grads[0], local_grads[1], local_grads[2]), 'tok')  147 us
    unnamed x4, waiting for transfers between devices  137 us
    dot_general x36, matrix products, contract_cols(): lax.dot_general(first_op, second_op, (((1,), (1,)), ((), ())), preferred_...  27.1 us
    reduce_sum x1, other arithmetic, local(): query_whole = jnp.sum(lax.all_gather(query_terms, 'tok'), axis=0)  20.5 us
  transfers between devices with their start and end apart: 3, of which 3 were waited for; matrix products, arithmetic and copies ran while one was open for 1% of the time, Pallas kernels for 0%

profile of v1, /device:TPU:0, one launch (start us, length us, event | category | flops | bytes accessed | tf_op | source)
XLA Modules:
  0.0 962.8 jit_solution(17140118895210348814)
XLA Ops:
  7.2 0.7 neg.32
  8.1 1.3 fusion.266
  9.5 1.6 fusion.272
  11.2 2.4 multiply_convert_fusion.2
  13.6 1.3 convolution_bitcast_fusion.8
  14.9 1.3 convolution_bitcast_fusion.7
  16.2 1.4 convolution_bitcast_fusion.6
  17.7 1.0 copy.159
  18.7 1.1 copy.164
  19.8 1.0 copy.169
  20.8 146.9 %all-reduce.8.cloned.1.call-done = (f32[1,512,512]{1,2,0:T(8,128)}, f32[1,512,512]{1,2,0:T(8,128)}, f32[1,512,512]{1,2,0:T(8,128)}) async-done(((f32[1,512,512]{1,2,0:T(8,128)}, f32[1,512,512]{1,2,0:T(8,128)}, f32[1,512,512]{1,2,0:T(8,128)}), (f32[1,512,512]{1,2,0:T(8,128)}, f32[1,512,512]{1,2,0:T(8,128)}, f32[1,512,512]{1,2,0:T(8,128)})) %all-reduce.8.cloned.1.call-update) | async-done | bytes 3145744 | tf_op jit(solution)/shard_map/psum | solution.py:162
  167.7 2.1 multiply_reduce_fusion.5
  170.5 2.1 fusion.263
  172.7 1.1 copy-done.47
  175.9 0.8 copy-done.73
  177.7 1.3 fusion.26
  179.0 0.9 multiply_reduce_fusion.4
  181.0 1.0 copy-done.45
  182.5 0.8 copy-done.99
  184.7 0.8 copy-done.67
  186.5 1.2 fusion.29
  187.7 0.9 multiply_reduce_fusion.3
  192.0 1.0 copy-done.13
  193.4 0.8 copy-done.65
  195.8 0.5 fusion.36
  197.1 0.5 fusion.37
  197.7 1.2 multiply_convert_fusion.3
  198.8 0.5 fusion.38
  199.9 13.2 %all-reduce.2 = (f32[256]{0:T(256)S(1)}, f32[256]{0:T(256)S(1)}) all-reduce(f32[256]{0:T(256)S(1)} %get-tuple-element.39, f32[256]{0:T(256)S(1)} %multiply_reduce_fusion.6), channel_id=1, replica_groups=mesh['tok'=16,'head'=2] {'head'}, use_global_device_ids=true, to_apply=%region_9.0 | all-reduce | flops 512 | bytes 4096 | tf_op jit(solution)/shard_map/psum | solution.py:171
  213.6 1.5 multiply_convert_fusion
  216.5 2.4 copy.174
  219.2 507.7 %all-gather.3.cloned.1.call-done = f32[16,512,1536]{2,1,0:T(8,128)} async-done(((f32[1,512,1536]{2,1,0:T(8,128)}), f32[16,512,1536]{2,1,0:T(8,128)}) %all-gather.3.cloned.1.call-update) | async-done | bytes 50331664 | tf_op jit(solution)/shard_map/all_gather | solution.py:183
  726.9 20.5 %reduce.9 = f32[512,1536]{1,0:T(8,128)} reduce(f32[16,512,1536]{2,1,0:T(8,128)} %all-gather.3.cloned.1.call-done, f32[]{:T(128)} %constant.38.clone.1), dimensions={0}, to_apply=%region_10.0 | reduce | flops 11796480 | bytes 53477380 | tf_op jit(solution)/shard_map/reduce_sum | solution.py:183
  747.5 2.4 copy.175
  749.9 1.6 fusion.57
  751.4 1.8 convolution_convert_fusion.52
  764.9 0.5 fusion.107
  766.5 1.2 fusion.72
  767.7 1.3 convolution_convert_fusion.22
  771.2 0.6 fusion.135
  775.7 1.2 fusion.81
  777.0 1.3 convolution_convert_fusion.4
  779.7 2.1 multiply_reduce_fusion.2
  782.5 1.6 fusion.49
  784.1 1.7 fusion.103
  786.3 0.8 copy-done.52
  787.1 2.1 multiply_reduce_fusion.1
  789.9 3.0 fusion.172
  792.9 1.1 convolution_bitcast_fusion.19
  794.6 0.5 fusion.91
  795.5 0.8 copy-done.50
  796.3 1.3 multiply_reduce_fusion
  800.1 0.7 add_convert_fusion
  802.3 5.6 copy.205
  808.1 0.6 copy-done.106
  808.6 0.6 dynamic-slice.4
  809.9 1.3 fusion.455
  811.2 2.1 fusion.161
  814.4 1.0 fusion.160
  815.8 1.0 fusion.162
  816.8 136.5 %all-reduce.6.cloned.1.call-done = f32[1,512,1536]{2,0,1:T(1,128)} async-done(((f32[1,512,1536]{2,0,1:T(1,128)}), f32[1,512,1536]{2,0,1:T(1,128)}) %all-reduce.6.cloned.1.call-update) | async-done | bytes 3145744
  953.3 0.9 constant_dynamic-slice_fusion
  954.3 1.0 bitcast_add_fusion
  955.2 0.7 fusion.415
  (292 shorter events, 40.2 us)
Async XLA Ops:
  7.2 160.6 %all-reduce.8.cloned.1.call-start = ((), (), s32[]{:S(2)}) async-start(), calls=%async_computation.2 | async-start | bytes 6291456 | tf_op jit(solution)/shard_map/psum | solution.py:162
  9.5 5.4 copy-start.92
  11.1 5.1 copy-start.94
  11.1 5.1 copy-start.53
  13.6 2.6 copy-start.79
  13.6 2.6 copy-start.77
  13.6 2.6 copy-start.81
  14.9 2.8 copy-start.25
  16.2 2.5 copy-start.60
  16.2 3.6 copy-start.33
  17.6 709.3 %all-gather.3.cloned.1.call-start = ((), (), s32[]{:S(2)}) async-start(), calls=%async_computation | async-start | bytes 53477376 | tf_op jit(solution)/shard_map/all_gather | solution.py:183
  170.5 3.6 copy-start.37
  175.0 2.2 copy-start.11
  175.4 2.2 copy-start.21
  176.7 2.3 copy-start.40
  177.2 18.5 %copy-start.5 = (f32[1,512,512]{1,2,0:T(8,128)}, f32[1,512,512]{1,2,0:T(8,128)S(1)}, u32[]{:S(2)}) copy-start(f32[1,512,512]{1,2,0:T(8,128)S(1)} %fusion.10) | copy-start | bytes 3145732
  183.8 2.2 copy-start.9
  184.2 2.2 copy-start.15
  185.5 2.2 copy-start.35
  186.0 10.7 %copy-start.3 = (f32[1,512,512]{1,2,0:T(8,128)}, f32[1,512,512]{1,2,0:T(8,128)S(1)}, u32[]{:S(2)}) copy-start(f32[1,512,512]{1,2,0:T(8,128)S(1)} %fusion.15) | copy-start | bytes 3145732
  191.5 3.2 copy-start.7
  194.7 4.1 copy-start.1
  195.2 2.4 copy-start.17
  195.2 1.8 copy-start.71
  195.7 3.1 copy-start.69
  196.3 2.5 copy-start.27
  197.1 1.8 copy-start.62
  197.6 2.2 copy-start.56
  197.6 1.7 copy-start.86
  197.6 1.7 copy-start.105
  218.9 734.4 %all-reduce.6.cloned.1.call-start = ((), (), s32[]{:S(2)}) async-start(), calls=%async_computation.1 | async-start | bytes 6291456
  749.9 3.4 copy-start.24
  751.4 2.8 copy-start.6
  765.9 1.8 copy-start.41
  766.5 2.5 copy-start.51
  766.5 2.5 copy-start.70
  767.7 1.7 copy-start.2
  775.1 1.8 copy-start.36
  775.7 2.5 copy-start.49
  775.7 2.5 copy-start.48
  779.7 2.9 copy-start.46
  781.8 4.1 copy-start.42
  782.5 3.3 copy-start.104
  787.1 2.8 copy-start.39
  789.9 4.2 copy-start.44
  789.9 4.2 copy-start.76
  792.9 2.6 copy-start.29
  792.9 2.2 copy-start.103
  796.3 2.3 copy-start.54
  798.6 2.2 copy-start.31
  808.0 1.9 copy-start.28
  808.0 3.2 copy-start.57
  808.0 5.3 copy-start.30
  808.0 5.3 copy-start.82
  808.0 5.6 copy-start.59
  808.0 5.6 copy-start.80
  808.1 5.9 copy-start.26
  809.9 4.1 copy-start.85
  811.2 3.2 copy-start.61
  811.2 3.2 copy-start.91
  813.3 2.1 copy-start.32
  813.3 2.1 copy-start.78
  813.7 2.1 copy-start.34
  813.7 2.1 copy-start.89
  (47 other events, 52.6 us)
Sparse Core Ops, SparseCore 0:
  17.8 149.9 all-reduce.7
  219.1 507.8 all-gather.2
  808.2 145.1 all-reduce.5
